TPU v7x, 512 devices: a whole 4x8x8 slice. The times are simulated.
512 devices in a mesh: blk: 64 (over z_hi, y, core), rep: 8 (over z_lo, x).
Axes of the slice: x: 4, y: 8, z: 8 (z_hi: 4, z_lo: 2; z = z_hi * 2 + z_lo), core: 2. Of those that a mesh axis runs over, the one named last changes fastest.
Arguments:
- features: bfloat16 [32768, 128], P('blk'), may hold values from -6 to 6
- weight: bfloat16 [128, 256], replicated, may hold values from -0.5 to 0.5
- tile_vals: bfloat16 [64, 8, 8, 12, 128, 128], P('blk', 'rep'), may hold values from -0.0390625 to 0.0390625
- tile_pos: int32 [64, 8, 8, 12], P('blk', 'rep'), may hold values from 0 to 15, as said below
- tile_count: int32 [64, 8, 8], P('blk', 'rep'), may hold values from 1 to 12, as said below
- cotangent: bfloat16 [32768, 256], P(('blk', 'rep')), may hold values from -6 to 6
Outputs:
- activations: bfloat16 [32768, 256], P(('blk', 'rep'))
- feat_grad: bfloat16 [32768, 128], P(('blk', 'rep'))
- weight_grad: float32 [128, 256], replicated
Inputs may be any that keep to these rules, and one draw needn't show every extreme that they name: `tile_pos`: within one row group, copy and section the entries are distinct. `tile_count`: row group 0 has all 12 slots live in every copy and section.
All inputs are finite; a program needn't handle non-finite values.
Results may differ from a plain program's by a relative error of at most 0.014.
Values may be sent and summed in bfloat16 or wider, within the bound.
A program may use at most 128 MiB of HBM per device.

v0:
```python
import jax
import jax.numpy as jnp
from jax import lax
from jax.sharding import PartitionSpec as P


def passed_along(block, axis, distance):
    devices = range(lax.axis_size(axis))
    route = [((i - distance) % len(devices), i) for i in devices]
    return lax.ppermute(block, axis, route)


def gelu_tanh(value):
    return jax.nn.gelu(value, approximate=True)


def section_forward(tile_block, positions, live_count, current, blocks):
    tile_size = tile_block.shape[-1]
    columns = current.reshape(blocks, tile_size, current.shape[-1])
    picked = columns[positions % blocks]
    live_mask = (jnp.arange(tile_block.shape[0], dtype=jnp.int32) < live_count).astype(jnp.float32)
    product = jnp.einsum("tik,tkf->tif", tile_block, picked, preferred_element_type=jnp.float32)
    product = product * live_mask[:, None, None]
    placing = (
        (positions // blocks)[:, None] == jnp.arange(blocks, dtype=jnp.int32)[None, :]
    ).astype(jnp.float32)
    return jnp.einsum("tn,tif->nif", placing, product).reshape(
        blocks * tile_size, current.shape[-1]
    )


def section_backward(tile_block, positions, live_count, grad_rows, blocks):
    tile_size = tile_block.shape[-1]
    rows_view = grad_rows.reshape(blocks, tile_size, grad_rows.shape[-1])
    picked = rows_view[positions // blocks]
    live_mask = (jnp.arange(tile_block.shape[0], dtype=jnp.int32) < live_count).astype(jnp.float32)
    product = jnp.einsum("tki,tkf->tif", tile_block, picked, preferred_element_type=jnp.float32)
    product = product * live_mask[:, None, None]
    placing = (
        (positions % blocks)[:, None] == jnp.arange(blocks, dtype=jnp.int32)[None, :]
    ).astype(jnp.float32)
    return jnp.einsum("tn,tif->nif", placing, product).reshape(
        blocks * tile_size, grad_rows.shape[-1]
    )


def skew_forward(value, rep_index, rep_size):
    for bit_index in range((rep_size - 1).bit_length()):
        moved = passed_along(value, "blk", 1 << bit_index)
        value = jnp.where(jnp.right_shift(rep_index, bit_index) % 2 == 1, moved, value)
    return value


def skew_back(value, rep_index, rep_size):
    for bit_index in range((rep_size - 1).bit_length()):
        moved = passed_along(value, "blk", -(1 << bit_index))
        value = jnp.where(jnp.right_shift(rep_index, bit_index) % 2 == 1, moved, value)
    return value


def local(features, weight, tile_vals, tile_pos, tile_count, cotangent):
    rep_size = lax.axis_size("rep")
    rep_index = lax.axis_index("rep")
    local_tiles = tile_vals[0, 0]
    local_pos = tile_pos[0, 0]
    local_count = tile_count[0, 0]
    section_count = local_tiles.shape[0]
    tile_size = local_tiles.shape[-1]
    blocks = features.shape[0] // tile_size
    rows_share = features.shape[0] // rep_size
    row_start = rep_index * rows_share

    def section_terms(section, current):
        return section_forward(
            lax.dynamic_index_in_dim(local_tiles, section, 0, keepdims=False),
            lax.dynamic_index_in_dim(local_pos, section, 0, keepdims=False),
            lax.dynamic_index_in_dim(local_count, section, 0, keepdims=False),
            current,
            blocks,
        )

    hidden = jnp.dot(features, weight, preferred_element_type=jnp.float32).astype(jnp.bfloat16)
    seeded = skew_forward(hidden, rep_index, rep_size)
    zeros_total = jnp.zeros((features.shape[0], weight.shape[1]), jnp.float32)

    def one_step(section, state):
        current, total = state
        total = total + section_terms(section, current)
        current = passed_along(current, "blk", rep_size)
        return (current, total)

    current, total = lax.fori_loop(0, section_count - 1, one_step, (seeded, zeros_total))
    total = total + section_terms(section_count - 1, current)
    pre = lax.psum_scatter(total, "rep", scatter_dimension=0, tiled=True)
    outputs, pullback = jax.vjp(gelu_tanh, pre)
    activations = outputs.astype(jnp.bfloat16)
    pre_grad = pullback(cotangent.astype(jnp.float32))[0].astype(jnp.bfloat16)
    grad_rows = lax.all_gather(pre_grad, "rep", axis=0, tiled=True)

    def back_terms(section):
        return section_backward(
            lax.dynamic_index_in_dim(local_tiles, section, 0, keepdims=False),
            lax.dynamic_index_in_dim(local_pos, section, 0, keepdims=False),
            lax.dynamic_index_in_dim(local_count, section, 0, keepdims=False),
            grad_rows,
            blocks,
        )

    def back_step(section, carried):
        return passed_along(carried + back_terms(section), "blk", rep_size)

    carried = lax.fori_loop(0, section_count, back_step, zeros_total)
    carried = skew_back(carried, rep_index, rep_size)
    hidden_grad = lax.psum_scatter(carried, "rep", scatter_dimension=0, tiled=True).astype(
        jnp.bfloat16
    )
    feat_grad = lax.dot_general(
        hidden_grad, weight, (((1,), (1,)), ((), ())), preferred_element_type=jnp.float32
    ).astype(jnp.bfloat16)
    feat_rows = lax.dynamic_slice_in_dim(features, row_start, rows_share, 0)
    partial_grad = lax.dot_general(
        feat_rows, hidden_grad, (((0,), (0,)), ((), ())), preferred_element_type=jnp.float32
    )
    weight_grad = lax.psum(partial_grad, ("blk", "rep"))
    return (activations, feat_grad, weight_grad)


def solution(mesh):
    placed = (
        P("blk", None),
        P(),
        P("blk", "rep", None, None, None, None),
        P("blk", "rep", None, None),
        P("blk", "rep", None),
        P(("blk", "rep"), None),
    )
    return jax.shard_map(
        local,
        mesh=mesh,
        in_specs=placed,
        out_specs=(P(("blk", "rep"), None), P(("blk", "rep"), None), P()),
        check_vma=False,
    )
```

profile of v0, /device:TPU:1, one launch (start us, length us, event | category | flops | bytes accessed | tf_op | source)
XLA Modules:
  0.0 1005.6 jit_solution(1865556596306336657)
XLA Ops:
  9.1 4.6 collective-permute-start.2
  15.0 3.9 collective-permute-done.2
  18.9 1.9 collective-permute-start.3
  21.6 14.1 %collective-permute-done.3 = bf16[512,256]{1,0:T(8,128)(2,1)S(1)} collective-permute-done((bf16[512,256]{1,0:T(8,128)(2,1)S(1)}, bf16[512,256]{1,0:T(8,128)(2,1)S(1)}, u32[]{:S(2)}, u32[]{:S(2)}) %collective-permute-start.3) | collective-permute-done | bytes 262176 | tf_op jit(solution)/shard_map/ppermute | solution.py:10
  35.7 1.9 collective-permute-start.4
  38.4 12.9 %collective-permute-done.4 = bf16[512,256]{1,0:T(8,128)(2,1)S(1)} collective-permute-done((bf16[512,256]{1,0:T(8,128)(2,1)S(1)}, bf16[512,256]{1,0:T(8,128)(2,1)S(1)}, u32[]{:S(2)}, u32[]{:S(2)}) %collective-permute-start.4) | collective-permute-done | bytes 262176 | tf_op jit(solution)/shard_map/ppermute | solution.py:10
  51.4 140.1 %while.34 = (s32[]{:T(128)}, bf16[512,256]{1,0:T(8,128)(2,1)S(1)}, f32[512,256]{1,0:T(8,128)S(1)}, s32[8,12]{1,0:T(8,128)S(1)}, bf16[8,12,128,128]{3,2,1,0:T(8,1...) while((s32[]{:T(128)}, bf16[512,256]{1,0:T(8,128)(2,1)S(1)}, f32[512,256]{1,0:T(8,128)S(1)}, ...), condition=%wide.region_1.2_spmd.clone, body=%wide.region_0.1_spmd.clone.sunk | while | flops 104465824 | bytes 10621531 | solution.py:92
  51.4 1.9 collective-permute-start.1
  55.2 1.4 fusion.77
  57.8 10.0 collective-permute-done.1
  67.8 1.9 collective-permute-start.1
  74.2 13.7 %collective-permute-done.1 = bf16[512,256]{1,0:T(8,128)(2,1)S(1)} collective-permute-done((bf16[512,256]{1,0:T(8,128)(2,1)S(1)}, bf16[512,256]{1,0:T(8,128)(2,1)S(1)}, u32[]{:S(2)}, u32[]{:S(2)}) %collective-permute-start.1) | collective-permute-done | bytes 262176 | tf_op jit(solution)/shard_map/while/body/eval_jaxpr/ppermute | solution.py:10
  87.9 1.9 collective-permute-start.1
  94.3 14.5 %collective-permute-done.1 = bf16[512,256]{1,0:T(8,128)(2,1)S(1)} collective-permute-done((bf16[512,256]{1,0:T(8,128)(2,1)S(1)}, bf16[512,256]{1,0:T(8,128)(2,1)S(1)}, u32[]{:S(2)}, u32[]{:S(2)}) %collective-permute-start.1) | collective-permute-done | bytes 262176 | tf_op jit(solution)/shard_map/while/body/eval_jaxpr/ppermute | solution.py:10
  108.8 1.9 collective-permute-start.1
  115.2 14.4 %collective-permute-done.1 = bf16[512,256]{1,0:T(8,128)(2,1)S(1)} collective-permute-done((bf16[512,256]{1,0:T(8,128)(2,1)S(1)}, bf16[512,256]{1,0:T(8,128)(2,1)S(1)}, u32[]{:S(2)}, u32[]{:S(2)}) %collective-permute-start.1) | collective-permute-done | bytes 262176 | tf_op jit(solution)/shard_map/while/body/eval_jaxpr/ppermute | solution.py:10
  129.6 1.9 collective-permute-start.1
  136.0 14.3 %collective-permute-done.1 = bf16[512,256]{1,0:T(8,128)(2,1)S(1)} collective-permute-done((bf16[512,256]{1,0:T(8,128)(2,1)S(1)}, bf16[512,256]{1,0:T(8,128)(2,1)S(1)}, u32[]{:S(2)}, u32[]{:S(2)}) %collective-permute-start.1) | collective-permute-done | bytes 262176 | tf_op jit(solution)/shard_map/while/body/eval_jaxpr/ppermute | solution.py:10
  150.3 2.6 collective-permute-start.1
  154.8 1.4 fusion.77
  157.4 12.5 %collective-permute-done.1 = bf16[512,256]{1,0:T(8,128)(2,1)S(1)} collective-permute-done((bf16[512,256]{1,0:T(8,128)(2,1)S(1)}, bf16[512,256]{1,0:T(8,128)(2,1)S(1)}, u32[]{:S(2)}, u32[]{:S(2)}) %collective-permute-start.1) | collective-permute-done | bytes 262176 | tf_op jit(solution)/shard_map/while/body/eval_jaxpr/ppermute | solution.py:10
  169.9 3.7 collective-permute-start.1
  178.1 13.4 %collective-permute-done.1 = bf16[512,256]{1,0:T(8,128)(2,1)S(1)} collective-permute-done((bf16[512,256]{1,0:T(8,128)(2,1)S(1)}, bf16[512,256]{1,0:T(8,128)(2,1)S(1)}, u32[]{:S(2)}, u32[]{:S(2)}) %collective-permute-start.1) | collective-permute-done | bytes 262176 | tf_op jit(solution)/shard_map/while/body/eval_jaxpr/ppermute | solution.py:10
  192.1 2.6 fusion.26
  194.7 2.2 copy.14
  198.3 52.4 %reduce-scatter.3.cloned.1.call-done = f32[64,256]{1,0:T(8,128)} async-done(((f32[512,256]{1,0:T(8,128)}), f32[64,256]{1,0:T(8,128)}) %reduce-scatter.3.cloned.1.call-update) | async-done | bytes 65552 | tf_op jit(solution)/shard_map/reduce_scatter | solution.py:94
  250.7 1.5 fusion.31
  252.2 22.0 %all_gather.3 = bf16[512,256]{1,0:T(8,128)(2,1)S(1)} all-gather(bf16[64,256]{1,0:T(8,128)(2,1)S(1)} %get-tuple-element.366), channel_id=1, replica_groups=mesh['blk'=64,'rep'=8] {'rep'}, dimensions={0}, use_global_device_ids=true | all-gather | bytes 294912 | tf_op jit(solution)/shard_map/all_gather | solution.py:98
  274.2 247.6 %while.33 = (s32[]{:T(128)}, f32[512,256]{1,0:T(8,128)S(1)}, s32[8,12]{1,0:T(8,128)S(1)}, bf16[8,12,128,128]{3,2,1,0:T(8,128)(2,1)}, bf16[512,256]{1,0:T(8,128)(2,1)S(1)}, /*index=5*/s32[8]{0:T(128)S(1)}, s32[]{:T(128)}) while((s32[]{:T(128)}, f32[512,256]{1,0:T(8,128)S(1)}, s32[8,12]{1,0:T(8,128)S(1)}, bf16[8,12,128,128]{3,2,1,0:T(8,128)(2,1)}, ...), condition=%wide.region_4.5_spmd, body=%wide.region_3.4_spmd.sunk | while | flops 104334752 | bytes 11146301 | solution.py:112
  276.2 1.4 fusion.71
  278.7 6.7 collective-permute-start
  285.5 15.3 %collective-permute-done = f32[512,256]{1,0:T(8,128)S(1)} collective-permute-done((f32[512,256]{1,0:T(8,128)S(1)}, f32[512,256]{1,0:T(8,128)S(1)}, u32[]{:S(2)}, u32[]{:S(2)}) %collective-permute-start) | collective-permute-done | bytes 524320 | tf_op jit(solution)/shard_map/while/body/eval_jaxpr/ppermute | solution.py:10
  302.7 1.4 fusion.71
  305.3 1.9 collective-permute-start
  307.2 23.0 %collective-permute-done = f32[512,256]{1,0:T(8,128)S(1)} collective-permute-done((f32[512,256]{1,0:T(8,128)S(1)}, f32[512,256]{1,0:T(8,128)S(1)}, u32[]{:S(2)}, u32[]{:S(2)}) %collective-permute-start) | collective-permute-done | bytes 524320 | tf_op jit(solution)/shard_map/while/body/eval_jaxpr/ppermute | solution.py:10
  332.2 1.4 fusion.71
  334.7 1.9 collective-permute-start
  336.7 28.7 %collective-permute-done = f32[512,256]{1,0:T(8,128)S(1)} collective-permute-done((f32[512,256]{1,0:T(8,128)S(1)}, f32[512,256]{1,0:T(8,128)S(1)}, u32[]{:S(2)}, u32[]{:S(2)}) %collective-permute-start) | collective-permute-done | bytes 524320 | tf_op jit(solution)/shard_map/while/body/eval_jaxpr/ppermute | solution.py:10
  367.3 1.4 fusion.71
  369.8 1.9 collective-permute-start
  371.8 27.3 %collective-permute-done = f32[512,256]{1,0:T(8,128)S(1)} collective-permute-done((f32[512,256]{1,0:T(8,128)S(1)}, f32[512,256]{1,0:T(8,128)S(1)}, u32[]{:S(2)}, u32[]{:S(2)}) %collective-permute-start) | collective-permute-done | bytes 524320 | tf_op jit(solution)/shard_map/while/body/eval_jaxpr/ppermute | solution.py:10
  400.9 1.4 fusion.71
  403.5 1.9 collective-permute-start
  405.4 26.0 %collective-permute-done = f32[512,256]{1,0:T(8,128)S(1)} collective-permute-done((f32[512,256]{1,0:T(8,128)S(1)}, f32[512,256]{1,0:T(8,128)S(1)}, u32[]{:S(2)}, u32[]{:S(2)}) %collective-permute-start) | collective-permute-done | bytes 524320 | tf_op jit(solution)/shard_map/while/body/eval_jaxpr/ppermute | solution.py:10
  433.3 1.4 fusion.71
  435.9 1.9 collective-permute-start
  437.8 26.0 %collective-permute-done = f32[512,256]{1,0:T(8,128)S(1)} collective-permute-done((f32[512,256]{1,0:T(8,128)S(1)}, f32[512,256]{1,0:T(8,128)S(1)}, u32[]{:S(2)}, u32[]{:S(2)}) %collective-permute-start) | collective-permute-done | bytes 524320 | tf_op jit(solution)/shard_map/while/body/eval_jaxpr/ppermute | solution.py:10
  465.7 1.4 fusion.71
  468.3 1.9 collective-permute-start
  470.2 20.2 %collective-permute-done = f32[512,256]{1,0:T(8,128)S(1)} collective-permute-done((f32[512,256]{1,0:T(8,128)S(1)}, f32[512,256]{1,0:T(8,128)S(1)}, u32[]{:S(2)}, u32[]{:S(2)}) %collective-permute-start) | collective-permute-done | bytes 524320 | tf_op jit(solution)/shard_map/while/body/eval_jaxpr/ppermute | solution.py:10
  492.3 1.4 fusion.71
  494.9 1.9 collective-permute-start
  496.8 25.0 %collective-permute-done = f32[512,256]{1,0:T(8,128)S(1)} collective-permute-done((f32[512,256]{1,0:T(8,128)S(1)}, f32[512,256]{1,0:T(8,128)S(1)}, u32[]{:S(2)}, u32[]{:S(2)}) %collective-permute-start) | collective-permute-done | bytes 524320 | tf_op jit(solution)/shard_map/while/body/eval_jaxpr/ppermute | solution.py:10
  521.8 27.2 %collective-permute-start.5 = (f32[512,256]{1,0:T(8,128)S(1)}, f32[512,256]{1,0:T(8,128)S(1)}, u32[]{:S(2)}, u32[]{:S(2)}) collective-permute-start(f32[512,256]{1,0:T(8,128)S(1)} %get-tuple-element.320), channel_id=1, source_target_pairs={{8,0},{16,8},{24,16},{32,24},{40,32},{48,40},{56,48},{64,56},{72,6... | collective-permute-start | bytes 1572872 | tf_op jit(solution)/shard_map/ppermute | solution.py:10
  549.0 1.5 collective-permute-done.5
  550.6 17.8 %collective-permute-start.6 = (f32[512,256]{1,0:T(8,128)S(1)}, f32[512,256]{1,0:T(8,128)S(1)}, u32[]{:S(2)}, u32[]{:S(2)}) collective-permute-start(f32[512,256]{1,0:T(8,128)S(1)} %broadcast_select_fusion), channel_id=1, source_target_pairs={{16,0},{24,8},{32,16},{40,24},{48,32},{56,40},{64,48},{72,56},{80,... | collective-permute-start | bytes 1572872 | tf_op jit(solution)/shard_map/ppermute | solution.py:10
  568.4 70.9 %collective-permute-done.6 = f32[512,256]{1,0:T(8,128)S(1)} collective-permute-done((f32[512,256]{1,0:T(8,128)S(1)}, f32[512,256]{1,0:T(8,128)S(1)}, u32[]{:S(2)}, u32[]{:S(2)}) %collective-permute-start.6) | collective-permute-done | bytes 524320 | tf_op jit(solution)/shard_map/ppermute | solution.py:10
  639.3 3.4 collective-permute-start.7
  642.8 19.5 %collective-permute-done.7 = f32[512,256]{1,0:T(8,128)S(1)} collective-permute-done((f32[512,256]{1,0:T(8,128)S(1)}, f32[512,256]{1,0:T(8,128)S(1)}, u32[]{:S(2)}, u32[]{:S(2)}) %collective-permute-start.7) | collective-permute-done | bytes 524320 | tf_op jit(solution)/shard_map/ppermute | solution.py:10
  663.2 59.4 %reduce-scatter.5.cloned.1.call-done = f32[64,256]{1,0:T(8,128)} async-done(((f32[512,256]{1,0:T(8,128)}), f32[64,256]{1,0:T(8,128)}) %reduce-scatter.5.cloned.1.call-update) | async-done | bytes 65552 | tf_op jit(solution)/shard_map/reduce_scatter | solution.py:114
  722.7 1.7 fusion.39
  724.4 1.6 convolution_convert_fusion.1
  726.0 271.6 %all-reduce.2.cloned.1.call-done = f32[128,256]{1,0:T(8,128)} async-done(((f32[128,256]{1,0:T(8,128)}), f32[128,256]{1,0:T(8,128)}) %all-reduce.2.cloned.1.call-update) | async-done | bytes 131088 | tf_op jit(solution)/shard_map/psum | solution.py:124
  997.6 1.6 copy.43
  (181 shorter events, 60.1 us)
Async XLA Ops:
  7.2 0.9 copy-start
  7.2 44.2 %copy-start.4 = (s32[1,1,8]{2,1,0:T(1,128)S(1)}, s32[1,1,8]{2,1,0:T(1,128)}, u32[]{:S(2)}) copy-start(s32[1,1,8]{2,1,0:T(1,128)} %param.14) | copy-start | bytes 100
  7.2 31.2 %copy-start.3 = (s32[1,1,8,12]{3,2,1,0:T(8,128)S(1)}, s32[1,1,8,12]{3,2,1,0:T(8,128)}, u32[]{:S(2)}) copy-start(s32[1,1,8,12]{3,2,1,0:T(8,128)} %param.13) | copy-start | bytes 1156
  7.2 243.5 %reduce-scatter.3.cloned.1.call-start = ((), (), s32[]{:S(2)}) async-start(), calls=%async_computation.2 | async-start | bytes 589824 | tf_op jit(solution)/shard_map/reduce_scatter | solution.py:94
  9.1 9.8 collective-permute-start.2
  18.9 16.8 %collective-permute-start.3 = (bf16[512,256]{1,0:T(8,128)(2,1)S(1)}, bf16[512,256]{1,0:T(8,128)(2,1)S(1)}, u32[]{:S(2)}, u32[]{:S(2)}) collective-permute-start(bf16[512,256]{1,0:T(8,128)(2,1)S(1)} %broadcast_select_fusion.1), channel_id=1, source_target_pairs={{496,0},{504,8},{0,16},{8,24},{16,32},{24,40},{32,48},{40,56},{48,... | collective-permute-start | bytes 786440 | tf_op jit(solution)/shard_map/ppermute | solution.py:10
  35.7 15.6 %collective-permute-start.4 = (bf16[512,256]{1,0:T(8,128)(2,1)S(1)}, bf16[512,256]{1,0:T(8,128)(2,1)S(1)}, u32[]{:S(2)}, u32[]{:S(2)}) collective-permute-start(bf16[512,256]{1,0:T(8,128)(2,1)S(1)} %broadcast_select_fusion.3), channel_id=1, source_target_pairs={{480,0},{488,8},{496,16},{504,24},{0,32},{8,40},{16,48},{24,56},{3... | collective-permute-start | bytes 786440 | tf_op jit(solution)/shard_map/ppermute | solution.py:10
  51.4 16.4 %collective-permute-start.1 = (bf16[512,256]{1,0:T(8,128)(2,1)S(1)}, bf16[512,256]{1,0:T(8,128)(2,1)S(1)}, u32[]{:S(2)}, u32[]{:S(2)}) collective-permute-start(bf16[512,256]{1,0:T(8,128)(2,1)S(1)} %copy.31), channel_id=1, source_target_pairs={{448,0},{456,8},{464,16},{472,24},{480,32},{488,40},{496,48},{504,... | collective-permute-start | bytes 786440 | tf_op jit(solution)/shard_map/while/body/eval_jaxpr/ppermute | solution.py:10
  67.8 20.1 %collective-permute-start.1 = (bf16[512,256]{1,0:T(8,128)(2,1)S(1)}, bf16[512,256]{1,0:T(8,128)(2,1)S(1)}, u32[]{:S(2)}, u32[]{:S(2)}) collective-permute-start(bf16[512,256]{1,0:T(8,128)(2,1)S(1)} %copy.31), channel_id=1, source_target_pairs={{448,0},{456,8},{464,16},{472,24},{480,32},{488,40},{496,48},{504,... | collective-permute-start | bytes 786440 | tf_op jit(solution)/shard_map/while/body/eval_jaxpr/ppermute | solution.py:10
  87.9 20.9 %collective-permute-start.1 = (bf16[512,256]{1,0:T(8,128)(2,1)S(1)}, bf16[512,256]{1,0:T(8,128)(2,1)S(1)}, u32[]{:S(2)}, u32[]{:S(2)}) collective-permute-start(bf16[512,256]{1,0:T(8,128)(2,1)S(1)} %copy.31), channel_id=1, source_target_pairs={{448,0},{456,8},{464,16},{472,24},{480,32},{488,40},{496,48},{504,... | collective-permute-start | bytes 786440 | tf_op jit(solution)/shard_map/while/body/eval_jaxpr/ppermute | solution.py:10
  108.8 20.8 %collective-permute-start.1 = (bf16[512,256]{1,0:T(8,128)(2,1)S(1)}, bf16[512,256]{1,0:T(8,128)(2,1)S(1)}, u32[]{:S(2)}, u32[]{:S(2)}) collective-permute-start(bf16[512,256]{1,0:T(8,128)(2,1)S(1)} %copy.31), channel_id=1, source_target_pairs={{448,0},{456,8},{464,16},{472,24},{480,32},{488,40},{496,48},{504,... | collective-permute-start | bytes 786440 | tf_op jit(solution)/shard_map/while/body/eval_jaxpr/ppermute | solution.py:10
  129.6 20.7 %collective-permute-start.1 = (bf16[512,256]{1,0:T(8,128)(2,1)S(1)}, bf16[512,256]{1,0:T(8,128)(2,1)S(1)}, u32[]{:S(2)}, u32[]{:S(2)}) collective-permute-start(bf16[512,256]{1,0:T(8,128)(2,1)S(1)} %copy.31), channel_id=1, source_target_pairs={{448,0},{456,8},{464,16},{472,24},{480,32},{488,40},{496,48},{504,... | collective-permute-start | bytes 786440 | tf_op jit(solution)/shard_map/while/body/eval_jaxpr/ppermute | solution.py:10
  150.3 19.5 %collective-permute-start.1 = (bf16[512,256]{1,0:T(8,128)(2,1)S(1)}, bf16[512,256]{1,0:T(8,128)(2,1)S(1)}, u32[]{:S(2)}, u32[]{:S(2)}) collective-permute-start(bf16[512,256]{1,0:T(8,128)(2,1)S(1)} %copy.31), channel_id=1, source_target_pairs={{448,0},{456,8},{464,16},{472,24},{480,32},{488,40},{496,48},{504,... | collective-permute-start | bytes 786440 | tf_op jit(solution)/shard_map/while/body/eval_jaxpr/ppermute | solution.py:10
  169.9 21.6 %collective-permute-start.1 = (bf16[512,256]{1,0:T(8,128)(2,1)S(1)}, bf16[512,256]{1,0:T(8,128)(2,1)S(1)}, u32[]{:S(2)}, u32[]{:S(2)}) collective-permute-start(bf16[512,256]{1,0:T(8,128)(2,1)S(1)} %copy.31), channel_id=1, source_target_pairs={{448,0},{456,8},{464,16},{472,24},{480,32},{488,40},{496,48},{504,... | collective-permute-start | bytes 786440 | tf_op jit(solution)/shard_map/while/body/eval_jaxpr/ppermute | solution.py:10
  197.2 53.4 %copy-start.2 = (bf16[64,256]{1,0:T(8,128)(2,1)S(1)}, bf16[64,256]{1,0:T(8,128)(2,1)}, u32[]{:S(2)}) copy-start(bf16[64,256]{1,0:T(8,128)(2,1)} %param.15) | copy-start | bytes 98308
  198.3 524.4 %reduce-scatter.5.cloned.1.call-start = ((), (), s32[]{:S(2)}) async-start(), calls=%async_computation.3 | async-start | bytes 589824 | tf_op jit(solution)/shard_map/reduce_scatter | solution.py:114
  278.7 22.1 %collective-permute-start = (f32[512,256]{1,0:T(8,128)S(1)}, f32[512,256]{1,0:T(8,128)S(1)}, u32[]{:S(2)}, u32[]{:S(2)}) collective-permute-start(f32[512,256]{1,0:T(8,128)S(1)} %bitcast_add_fusion.5), channel_id=1, source_target_pairs={{448,0},{456,8},{464,16},{472,24},{480,32},{488,40},{496,48},{504,... | collective-permute-start | bytes 1572872 | tf_op jit(solution)/shard_map/while/body/eval_jaxpr/ppermute | solution.py:10
  305.3 25.0 %collective-permute-start = (f32[512,256]{1,0:T(8,128)S(1)}, f32[512,256]{1,0:T(8,128)S(1)}, u32[]{:S(2)}, u32[]{:S(2)}) collective-permute-start(f32[512,256]{1,0:T(8,128)S(1)} %bitcast_add_fusion.5), channel_id=1, source_target_pairs={{448,0},{456,8},{464,16},{472,24},{480,32},{488,40},{496,48},{504,... | collective-permute-start | bytes 1572872 | tf_op jit(solution)/shard_map/while/body/eval_jaxpr/ppermute | solution.py:10
  334.7 30.6 %collective-permute-start = (f32[512,256]{1,0:T(8,128)S(1)}, f32[512,256]{1,0:T(8,128)S(1)}, u32[]{:S(2)}, u32[]{:S(2)}) collective-permute-start(f32[512,256]{1,0:T(8,128)S(1)} %bitcast_add_fusion.5), channel_id=1, source_target_pairs={{448,0},{456,8},{464,16},{472,24},{480,32},{488,40},{496,48},{504,... | collective-permute-start | bytes 1572872 | tf_op jit(solution)/shard_map/while/body/eval_jaxpr/ppermute | solution.py:10
  369.8 29.2 %collective-permute-start = (f32[512,256]{1,0:T(8,128)S(1)}, f32[512,256]{1,0:T(8,128)S(1)}, u32[]{:S(2)}, u32[]{:S(2)}) collective-permute-start(f32[512,256]{1,0:T(8,128)S(1)} %bitcast_add_fusion.5), channel_id=1, source_target_pairs={{448,0},{456,8},{464,16},{472,24},{480,32},{488,40},{496,48},{504,... | collective-permute-start | bytes 1572872 | tf_op jit(solution)/shard_map/while/body/eval_jaxpr/ppermute | solution.py:10
  403.5 27.9 %collective-permute-start = (f32[512,256]{1,0:T(8,128)S(1)}, f32[512,256]{1,0:T(8,128)S(1)}, u32[]{:S(2)}, u32[]{:S(2)}) collective-permute-start(f32[512,256]{1,0:T(8,128)S(1)} %bitcast_add_fusion.5), channel_id=1, source_target_pairs={{448,0},{456,8},{464,16},{472,24},{480,32},{488,40},{496,48},{504,... | collective-permute-start | bytes 1572872 | tf_op jit(solution)/shard_map/while/body/eval_jaxpr/ppermute | solution.py:10
  435.9 28.0 %collective-permute-start = (f32[512,256]{1,0:T(8,128)S(1)}, f32[512,256]{1,0:T(8,128)S(1)}, u32[]{:S(2)}, u32[]{:S(2)}) collective-permute-start(f32[512,256]{1,0:T(8,128)S(1)} %bitcast_add_fusion.5), channel_id=1, source_target_pairs={{448,0},{456,8},{464,16},{472,24},{480,32},{488,40},{496,48},{504,... | collective-permute-start | bytes 1572872 | tf_op jit(solution)/shard_map/while/body/eval_jaxpr/ppermute | solution.py:10
  468.3 22.1 %collective-permute-start = (f32[512,256]{1,0:T(8,128)S(1)}, f32[512,256]{1,0:T(8,128)S(1)}, u32[]{:S(2)}, u32[]{:S(2)}) collective-permute-start(f32[512,256]{1,0:T(8,128)S(1)} %bitcast_add_fusion.5), channel_id=1, source_target_pairs={{448,0},{456,8},{464,16},{472,24},{480,32},{488,40},{496,48},{504,... | collective-permute-start | bytes 1572872 | tf_op jit(solution)/shard_map/while/body/eval_jaxpr/ppermute | solution.py:10
  494.9 27.0 %collective-permute-start = (f32[512,256]{1,0:T(8,128)S(1)}, f32[512,256]{1,0:T(8,128)S(1)}, u32[]{:S(2)}, u32[]{:S(2)}) collective-permute-start(f32[512,256]{1,0:T(8,128)S(1)} %bitcast_add_fusion.5), channel_id=1, source_target_pairs={{448,0},{456,8},{464,16},{472,24},{480,32},{488,40},{496,48},{504,... | collective-permute-start | bytes 1572872 | tf_op jit(solution)/shard_map/while/body/eval_jaxpr/ppermute | solution.py:10
  521.8 28.7 %collective-permute-start.5 = (f32[512,256]{1,0:T(8,128)S(1)}, f32[512,256]{1,0:T(8,128)S(1)}, u32[]{:S(2)}, u32[]{:S(2)}) collective-permute-start(f32[512,256]{1,0:T(8,128)S(1)} %get-tuple-element.320), channel_id=1, source_target_pairs={{8,0},{16,8},{24,16},{32,24},{40,32},{48,40},{56,48},{64,56},{72,6... | collective-permute-start | bytes 1572872 | tf_op jit(solution)/shard_map/ppermute | solution.py:10
  550.6 173.8 %copy-start.1 = (bf16[128,256]{1,0:T(8,128)(2,1)S(1)}, bf16[128,256]{1,0:T(8,128)(2,1)}, u32[]{:S(2)}) copy-start(bf16[128,256]{1,0:T(8,128)(2,1)} %param.11) | copy-start | bytes 196612
  550.6 88.7 %collective-permute-start.6 = (f32[512,256]{1,0:T(8,128)S(1)}, f32[512,256]{1,0:T(8,128)S(1)}, u32[]{:S(2)}, u32[]{:S(2)}) collective-permute-start(f32[512,256]{1,0:T(8,128)S(1)} %broadcast_select_fusion), channel_id=1, source_target_pairs={{16,0},{24,8},{32,16},{40,24},{48,32},{56,40},{64,48},{72,56},{80,... | collective-permute-start | bytes 1572872 | tf_op jit(solution)/shard_map/ppermute | solution.py:10
  639.3 22.9 %collective-permute-start.7 = (f32[512,256]{1,0:T(8,128)S(1)}, f32[512,256]{1,0:T(8,128)S(1)}, u32[]{:S(2)}, u32[]{:S(2)}) collective-permute-start(f32[512,256]{1,0:T(8,128)S(1)} %broadcast_select_fusion.2), channel_id=1, source_target_pairs={{32,0},{40,8},{48,16},{56,24},{64,32},{72,40},{80,48},{88,56},{96,... | collective-permute-start | bytes 1572872 | tf_op jit(solution)/shard_map/ppermute | solution.py:10
  663.2 334.4 %all-reduce.2.cloned.1.call-start = ((), (), s32[]{:S(2)}) async-start(), calls=%async_computation.4 | async-start | bytes 262144 | tf_op jit(solution)/shard_map/psum | solution.py:124
Sparse Core Ops, SparseCore 0:
  198.4 52.2 reduce-scatter.2
  663.3 59.3 reduce-scatter.4
  728.2 269.2 all-reduce.1
where the time goes:
time: 1010 us
  waiting for transfers between devices  791 us (78%)
  starting transfers between devices  93 us (9%)
  matrix products  42.5 us (4%)
  local copies, waits for them, and re-layouts  26.1 us (3%)
  blocking collectives  22 us (2%)
  other arithmetic  16.6 us (2%)
  between operations  14 us (1%)
    ppermute x21, waiting for transfers between devices, passed_along(): return lax.ppermute(block, axis, route)  407 us
    psum x1, waiting for transfers between devices, local(): weight_grad = lax.psum(partial_grad, ('blk', 'rep'))  272 us
    ppermute x21, starting transfers between devices, passed_along(): return lax.ppermute(block, axis, route)  92.9 us
    reduce_scatter x1, waiting for transfers between devices, local(): lax.psum_scatter(carried, 'rep', scatter_dimension=0, tiled=True)  59.4 us
    reduce_scatter x1, waiting for transfers between devices, local(): pre = lax.psum_scatter(total, 'rep', scatter_dimension=0, tiled=True)  52.4 us
    all_gather x1, blocking collectives, local(): grad_rows = lax.all_gather(pre_grad, 'rep', axis=0, tiled=True)  22 us
  transfers between devices with their start and end apart: 24, of which 24 were waited for; matrix products, arithmetic and copies ran while one was open for 3% of the time, Pallas kernels for 0%

commit v1 on v0

--- a/solution.py
+++ b/solution.py
@@ -121,7 +121,7 @@
     partial_grad = lax.dot_general(
         feat_rows, hidden_grad, (((0,), (0,)), ((), ())), preferred_element_type=jnp.float32
     )
-    weight_grad = lax.psum(partial_grad, ("blk", "rep"))
+    weight_grad = jnp.sum(lax.all_gather(partial_grad, ("blk", "rep")), axis=0)
     return (activations, feat_grad, weight_grad)
 
 

time: 1010 us -> 2260 us (2.24)
  waiting for transfers between devices: 791 us -> 2030 us
    all_gather x0 -> x1, waiting for transfers between devices: none -> 1500 us  [local(): weight_grad = jnp.sum(lax.all_gather(partial_grad, ('blk', 'rep')), axis=0)]
    psum x1 -> x0, waiting for transfers between devices: 272 us -> none  [local(): weight_grad = lax.psum(partial_grad, ('blk', 'rep'))]
  transfers between devices with their start and end apart: 24 -> 24, of which waited for: 24 -> 24; matrix products, arithmetic and copies ran while one was open for 3% -> 2% of each run, Pallas kernels for 0% -> 0%
where the time goes in v1:
time: 2260 us
  waiting for transfers between devices  2030 us (90%)
  starting transfers between devices  88.2 us (4%)
  matrix products  42.5 us (2%)
  other arithmetic  38.4 us (2%)
  local copies, waits for them, and re-layouts  24.5 us (1%)
    all_gather x1, waiting for transfers between devices, local(): weight_grad = jnp.sum(lax.all_gather(partial_grad, ('blk', 'rep')), axis=0)  1500 us
    ppermute x21, waiting for transfers between devices, passed_along(): return lax.ppermute(block, axis, route)  400 us
    ppermute x21, starting transfers between devices, passed_along(): return lax.ppermute(block, axis, route)  88.1 us
    reduce_scatter x1, waiting for transfers between devices, local(): lax.psum_scatter(carried, 'rep', scatter_dimension=0, tiled=True)  71.2 us
    reduce_scatter x1, waiting for transfers between devices, local(): pre = lax.psum_scatter(total, 'rep', scatter_dimension=0, tiled=True)  52.3 us
  transfers between devices with their start and end apart: 24, of which 24 were waited for; matrix products, arithmetic and copies ran while one was open for 2% of the time, Pallas kernels for 0%

profile of v1, /device:TPU:1, one launch (start us, length us, event | category | flops | bytes accessed | tf_op | source)
XLA Modules:
  0.0 2258.3 jit_solution(6768286756895917484)
XLA Ops:
  9.1 4.6 collective-permute-start.2
  15.0 3.9 collective-permute-done.2
  18.9 1.9 collective-permute-start.3
  21.6 14.1 collective-permute-done.3
  35.7 1.9 collective-permute-start.4
  38.4 12.9 collective-permute-done.4
  51.4 140.1 %while.34 = (s32[]{:T(128)}, bf16[512,256]{1,0:T(8,128)(2,1)S(1)}, f32[512,256]{1,0:T(8,128)S(1)}, s32[8,12]{1,0:T(8,128)S(1)}, bf16[8,12,128,128]{3,2,1,0:T(8,1...) while((s32[]{:T(128)}, bf16[512,256]{1,0:T(8,128)(2,1)S(1)}, f32[512,256]{1,0:T(8,128)S(1)}, ...), condition=%wide.region_1.2_spmd.clone, body=%wide.region_0.1_spmd.clone.sunk | while | flops 104465824 | bytes 10621531 | solution.py:92
  51.4 1.9 collective-permute-start.1
  57.8 10.0 collective-permute-done.1
  67.8 1.9 collective-permute-start.1
  74.2 13.7 collective-permute-done.1
  87.9 1.9 collective-permute-start.1
  91.8 1.4 fusion.77
  94.3 14.5 collective-permute-done.1
  108.8 1.9 collective-permute-start.1
  112.7 1.4 fusion.77
  115.2 14.4 collective-permute-done.1
  129.6 1.9 collective-permute-start.1
  136.0 14.3 collective-permute-done.1
  150.3 2.6 collective-permute-start.1
  157.4 12.5 collective-permute-done.1
  169.9 3.7 collective-permute-start.1
  178.1 13.4 collective-permute-done.1
  192.1 2.6 fusion.26
  194.7 2.2 copy.14
  198.3 52.3 %reduce-scatter.3.cloned.1.call-done = f32[64,256]{1,0:T(8,128)} async-done(((f32[512,256]{1,0:T(8,128)}), f32[64,256]{1,0:T(8,128)}) %reduce-scatter.3.cloned.1.call-update) | async-done | bytes 65552 | tf_op jit(solution)/shard_map/reduce_scatter | solution.py:94
  250.6 1.5 fusion.31
  252.1 22.0 all_gather.9
  274.2 241.4 %while.33 = (s32[]{:T(128)}, f32[512,256]{1,0:T(8,128)S(1)}, s32[8,12]{1,0:T(8,128)S(1)}, bf16[8,12,128,128]{3,2,1,0:T(8,128)(2,1)}, bf16[512,256]{1,0:T(8,128)(2,1)S(1)}, /*index=5*/s32[8]{0:T(128)S(1)}, s32[]{:T(128)}) while((s32[]{:T(128)}, f32[512,256]{1,0:T(8,128)S(1)}, s32[8,12]{1,0:T(8,128)S(1)}, bf16[8,12,128,128]{3,2,1,0:T(8,128)(2,1)}, ...), condition=%wide.region_4.5_spmd, body=%wide.region_3.4_spmd.sunk | while | flops 104334752 | bytes 11146301 | solution.py:112
  276.1 1.4 fusion.71
  278.7 6.7 collective-permute-start
  285.4 15.3 collective-permute-done
  302.7 1.4 fusion.71
  305.2 1.9 collective-permute-start
  307.2 22.8 %collective-permute-done = f32[512,256]{1,0:T(8,128)S(1)} collective-permute-done((f32[512,256]{1,0:T(8,128)S(1)}, f32[512,256]{1,0:T(8,128)S(1)}, u32[]{:S(2)}, u32[]{:S(2)}) %collective-permute-start) | collective-permute-done | bytes 524320 | tf_op jit(solution)/shard_map/while/body/eval_jaxpr/ppermute | solution.py:10
  331.8 1.4 fusion.71
  334.4 1.9 collective-permute-start
  336.3 28.2 %collective-permute-done = f32[512,256]{1,0:T(8,128)S(1)} collective-permute-done((f32[512,256]{1,0:T(8,128)S(1)}, f32[512,256]{1,0:T(8,128)S(1)}, u32[]{:S(2)}, u32[]{:S(2)}) %collective-permute-start) | collective-permute-done | bytes 524320 | tf_op jit(solution)/shard_map/while/body/eval_jaxpr/ppermute | solution.py:10
  366.4 1.4 fusion.71
  369.0 1.9 collective-permute-start
  370.9 26.1 %collective-permute-done = f32[512,256]{1,0:T(8,128)S(1)} collective-permute-done((f32[512,256]{1,0:T(8,128)S(1)}, f32[512,256]{1,0:T(8,128)S(1)}, u32[]{:S(2)}, u32[]{:S(2)}) %collective-permute-start) | collective-permute-done | bytes 524320 | tf_op jit(solution)/shard_map/while/body/eval_jaxpr/ppermute | solution.py:10
  398.9 1.4 fusion.71
  401.5 1.9 collective-permute-start
  403.4 21.2 collective-permute-done
  426.5 1.4 fusion.71
  429.1 1.9 collective-permute-start
  431.0 27.8 %collective-permute-done = f32[512,256]{1,0:T(8,128)S(1)} collective-permute-done((f32[512,256]{1,0:T(8,128)S(1)}, f32[512,256]{1,0:T(8,128)S(1)}, u32[]{:S(2)}, u32[]{:S(2)}) %collective-permute-start) | collective-permute-done | bytes 524320 | tf_op jit(solution)/shard_map/while/body/eval_jaxpr/ppermute | solution.py:10
  460.7 1.4 fusion.71
  463.3 1.9 collective-permute-start
  465.2 24.1 %collective-permute-done = f32[512,256]{1,0:T(8,128)S(1)} collective-permute-done((f32[512,256]{1,0:T(8,128)S(1)}, f32[512,256]{1,0:T(8,128)S(1)}, u32[]{:S(2)}, u32[]{:S(2)}) %collective-permute-start) | collective-permute-done | bytes 524320 | tf_op jit(solution)/shard_map/while/body/eval_jaxpr/ppermute | solution.py:10
  491.2 1.4 fusion.71
  493.8 1.9 collective-permute-start
  495.7 19.9 collective-permute-done
  515.6 26.1 %collective-permute-start.5 = (f32[512,256]{1,0:T(8,128)S(1)}, f32[512,256]{1,0:T(8,128)S(1)}, u32[]{:S(2)}, u32[]{:S(2)}) collective-permute-start(f32[512,256]{1,0:T(8,128)S(1)} %get-tuple-element.320), channel_id=1, source_target_pairs={{8,0},{16,8},{24,16},{32,24},{40,32},{48,40},{56,48},{64,56},{72,6... | collective-permute-start | bytes 1572872 | tf_op jit(solution)/shard_map/ppermute | solution.py:10
  541.7 1.5 collective-permute-done.5
  543.3 12.9 collective-permute-start.6
  556.2 72.5 %collective-permute-done.6 = f32[512,256]{1,0:T(8,128)S(1)} collective-permute-done((f32[512,256]{1,0:T(8,128)S(1)}, f32[512,256]{1,0:T(8,128)S(1)}, u32[]{:S(2)}, u32[]{:S(2)}) %collective-permute-start.6) | collective-permute-done | bytes 524320 | tf_op jit(solution)/shard_map/ppermute | solution.py:10
  628.8 4.6 collective-permute-start.7
  633.5 17.1 collective-permute-done.7
  651.4 71.2 %reduce-scatter.5.cloned.1.call-done = f32[64,256]{1,0:T(8,128)} async-done(((f32[512,256]{1,0:T(8,128)}), f32[64,256]{1,0:T(8,128)}) %reduce-scatter.5.cloned.1.call-update) | async-done | bytes 65552 | tf_op jit(solution)/shard_map/reduce_scatter | solution.py:114
  722.6 1.7 fusion.39
  724.3 1.6 convolution_convert_fusion.1
  725.9 1504.0 %all-gather.3.cloned.1.call-done = f32[65536,256]{1,0:T(8,128)} async-done(((f32[128,256]{1,0:T(8,128)}), f32[65536,256]{1,0:T(8,128)}) %all-gather.3.cloned.1.call-update) | async-done | bytes 67108880 | tf_op jit(solution)/shard_map/all_gather | solution.py:124
  2229.9 21.8 reduce_sum.9
  (181 shorter events, 60.0 us)
Async XLA Ops:
  7.2 0.9 copy-start
  7.2 44.2 %copy-start.4 = (s32[1,1,8]{2,1,0:T(1,128)S(1)}, s32[1,1,8]{2,1,0:T(1,128)}, u32[]{:S(2)}) copy-start(s32[1,1,8]{2,1,0:T(1,128)} %param.14) | copy-start | bytes 100
  7.2 31.2 %copy-start.3 = (s32[1,1,8,12]{3,2,1,0:T(8,128)S(1)}, s32[1,1,8,12]{3,2,1,0:T(8,128)}, u32[]{:S(2)}) copy-start(s32[1,1,8,12]{3,2,1,0:T(8,128)} %param.13) | copy-start | bytes 1156
  7.2 243.4 %reduce-scatter.3.cloned.1.call-start = ((), (), s32[]{:S(2)}) async-start(), calls=%async_computation.2 | async-start | bytes 589824 | tf_op jit(solution)/shard_map/reduce_scatter | solution.py:94
  9.1 9.8 collective-permute-start.2
  18.9 16.8 collective-permute-start.3
  35.7 15.6 collective-permute-start.4
  51.4 16.4 collective-permute-start.1
  67.8 20.1 collective-permute-start.1
  87.9 20.9 collective-permute-start.1
  108.8 20.8 collective-permute-start.1
  129.6 20.7 collective-permute-start.1
  150.3 19.6 collective-permute-start.1
  169.9 21.5 collective-permute-start.1
  197.2 53.4 %copy-start.2 = (bf16[64,256]{1,0:T(8,128)(2,1)S(1)}, bf16[64,256]{1,0:T(8,128)(2,1)}, u32[]{:S(2)}) copy-start(bf16[64,256]{1,0:T(8,128)(2,1)} %param.15) | copy-start | bytes 98308
  198.3 524.3 %reduce-scatter.5.cloned.1.call-start = ((), (), s32[]{:S(2)}) async-start(), calls=%async_computation.3 | async-start | bytes 589824 | tf_op jit(solution)/shard_map/reduce_scatter | solution.py:114
  278.7 22.1 collective-permute-start
  305.2 24.7 %collective-permute-start = (f32[512,256]{1,0:T(8,128)S(1)}, f32[512,256]{1,0:T(8,128)S(1)}, u32[]{:S(2)}, u32[]{:S(2)}) collective-permute-start(f32[512,256]{1,0:T(8,128)S(1)} %bitcast_add_fusion.5), channel_id=1, source_target_pairs={{448,0},{456,8},{464,16},{472,24},{480,32},{488,40},{496,48},{504,... | collective-permute-start | bytes 1572872 | tf_op jit(solution)/shard_map/while/body/eval_jaxpr/ppermute | solution.py:10
  334.4 30.1 %collective-permute-start = (f32[512,256]{1,0:T(8,128)S(1)}, f32[512,256]{1,0:T(8,128)S(1)}, u32[]{:S(2)}, u32[]{:S(2)}) collective-permute-start(f32[512,256]{1,0:T(8,128)S(1)} %bitcast_add_fusion.5), channel_id=1, source_target_pairs={{448,0},{456,8},{464,16},{472,24},{480,32},{488,40},{496,48},{504,... | collective-permute-start | bytes 1572872 | tf_op jit(solution)/shard_map/while/body/eval_jaxpr/ppermute | solution.py:10
  369.0 28.0 %collective-permute-start = (f32[512,256]{1,0:T(8,128)S(1)}, f32[512,256]{1,0:T(8,128)S(1)}, u32[]{:S(2)}, u32[]{:S(2)}) collective-permute-start(f32[512,256]{1,0:T(8,128)S(1)} %bitcast_add_fusion.5), channel_id=1, source_target_pairs={{448,0},{456,8},{464,16},{472,24},{480,32},{488,40},{496,48},{504,... | collective-permute-start | bytes 1572872 | tf_op jit(solution)/shard_map/while/body/eval_jaxpr/ppermute | solution.py:10
  401.5 23.1 %collective-permute-start = (f32[512,256]{1,0:T(8,128)S(1)}, f32[512,256]{1,0:T(8,128)S(1)}, u32[]{:S(2)}, u32[]{:S(2)}) collective-permute-start(f32[512,256]{1,0:T(8,128)S(1)} %bitcast_add_fusion.5), channel_id=1, source_target_pairs={{448,0},{456,8},{464,16},{472,24},{480,32},{488,40},{496,48},{504,... | collective-permute-start | bytes 1572872 | tf_op jit(solution)/shard_map/while/body/eval_jaxpr/ppermute | solution.py:10
  429.1 29.7 %collective-permute-start = (f32[512,256]{1,0:T(8,128)S(1)}, f32[512,256]{1,0:T(8,128)S(1)}, u32[]{:S(2)}, u32[]{:S(2)}) collective-permute-start(f32[512,256]{1,0:T(8,128)S(1)} %bitcast_add_fusion.5), channel_id=1, source_target_pairs={{448,0},{456,8},{464,16},{472,24},{480,32},{488,40},{496,48},{504,... | collective-permute-start | bytes 1572872 | tf_op jit(solution)/shard_map/while/body/eval_jaxpr/ppermute | solution.py:10
  463.3 26.0 %collective-permute-start = (f32[512,256]{1,0:T(8,128)S(1)}, f32[512,256]{1,0:T(8,128)S(1)}, u32[]{:S(2)}, u32[]{:S(2)}) collective-permute-start(f32[512,256]{1,0:T(8,128)S(1)} %bitcast_add_fusion.5), channel_id=1, source_target_pairs={{448,0},{456,8},{464,16},{472,24},{480,32},{488,40},{496,48},{504,... | collective-permute-start | bytes 1572872 | tf_op jit(solution)/shard_map/while/body/eval_jaxpr/ppermute | solution.py:10
  493.8 21.8 collective-permute-start
  515.6 27.6 %collective-permute-start.5 = (f32[512,256]{1,0:T(8,128)S(1)}, f32[512,256]{1,0:T(8,128)S(1)}, u32[]{:S(2)}, u32[]{:S(2)}) collective-permute-start(f32[512,256]{1,0:T(8,128)S(1)} %get-tuple-element.320), channel_id=1, source_target_pairs={{8,0},{16,8},{24,16},{32,24},{40,32},{48,40},{56,48},{64,56},{72,6... | collective-permute-start | bytes 1572872 | tf_op jit(solution)/shard_map/ppermute | solution.py:10
  543.3 181.1 %copy-start.1 = (bf16[128,256]{1,0:T(8,128)(2,1)S(1)}, bf16[128,256]{1,0:T(8,128)(2,1)}, u32[]{:S(2)}) copy-start(bf16[128,256]{1,0:T(8,128)(2,1)} %param.11) | copy-start | bytes 196612
  543.3 85.5 %collective-permute-start.6 = (f32[512,256]{1,0:T(8,128)S(1)}, f32[512,256]{1,0:T(8,128)S(1)}, u32[]{:S(2)}, u32[]{:S(2)}) collective-permute-start(f32[512,256]{1,0:T(8,128)S(1)} %broadcast_select_fusion), channel_id=1, source_target_pairs={{16,0},{24,8},{32,16},{40,24},{48,32},{56,40},{64,48},{72,56},{80,... | collective-permute-start | bytes 1572872 | tf_op jit(solution)/shard_map/ppermute | solution.py:10
  628.8 21.7 collective-permute-start.7
  651.4 1578.5 %all-gather.3.cloned.1.call-start = ((), (), s32[]{:S(2)}) async-start(), calls=%async_computation.4 | async-start | bytes 67239936 | tf_op jit(solution)/shard_map/all_gather | solution.py:124
Sparse Core Ops, SparseCore 0:
  198.4 52.2 reduce-scatter.2
  651.5 71.0 reduce-scatter.4
  725.4 1504.4 all-gather.2
